TPU v7x, 512 devices: a whole 4x8x8 slice. The times are simulated.
512 devices in a mesh: req: 64 (over y, x, core), tp: 8 (over z).
Axes of the slice: x: 4, y: 8, z: 8, core: 2. Of those that a mesh axis runs over, the one named last changes fastest.
Arguments:
- tokens: bfloat16 [13312, 2048], P('req', 'tp'), may hold values from -6 to 6
- ln_gain: bfloat16 [2048], P('tp'), may hold values from 0.099609375 to 1.8984375
- ln_bias: bfloat16 [2048], P('tp'), may hold values from -3 to 3
- w_qkv: bfloat16 [2048, 3, 1024], P(None, None, 'tp'), may hold values from -3 to 3
- qkv_bias: bfloat16 [3, 1024], P(None, 'tp'), may hold values from -3 to 3
- w_dense: bfloat16 [1024, 2048], P('tp'), may hold values from -0.1875 to 0.1875
- dense_bias: bfloat16 [2048], P('tp'), may hold values from -3 to 3
- prefix_kv: bfloat16 [1024, 32, 2, 1024], P('req', None, None, 'tp'), may hold values from -6 to 6
- lengths: int32 [64, 16], replicated, may hold values from 1 to 16, 208 in all within a row
- owner_slot: int32 [1024], replicated, may hold values from 0 to 1023, as said below
Outputs:
- attended: bfloat16 [13312, 2048], P('req', 'tp')
- new_cache: bfloat16 [1024, 16, 2, 1024], P('req', None, None, 'tp')
Inputs may be any that keep to these rules, and one draw needn't show every extreme that they name: owner_slot names every slot once; owner_slot[g] % 16 == g % 16; two requests of one req index name slots on the same req index only if their j differ by a multiple of 64, so one req index sends exactly 1 request to each req index that it sends to. `lengths`: each row sums to 208 and reaches 16.
All inputs are finite; a program needn't handle non-finite values.
Results may differ from a plain program's by a relative error of at most 0.014.
Values may be sent and summed in bfloat16 or wider, within the bound.
No kernel may reach another device: no remote copies, remote signals or barrier semaphores. Data moves between devices by JAX's collectives and lax.ppermute only.
A program may use at most 64 MiB of HBM per device.

v0:
```python
import math
import jax
import jax.numpy as jnp
from jax import lax
from jax.sharding import PartitionSpec as P

D = 2048
HD = 128
HEADS = 8
LMAX = 16
PRE = 32


def moments_norm(values, total_one, total_two, gain_vec, shift_vec, width):
    mean_val = total_one[:, None] / width
    second = total_two[:, None] / width
    scale_inv = lax.rsqrt(second - mean_val * mean_val + 1e-05)
    return (
        (values - mean_val) * scale_inv * gain_vec.astype(jnp.float32)
        + shift_vec.astype(jnp.float32)
    ).astype(jnp.bfloat16)


def bucket_table(targets, count):
    return (targets[None, :] == jnp.arange(count, dtype=jnp.int32)[:, None]).astype(jnp.int32)


def attend(queries, all_keys, all_values, slopes, prefix_len):
    span = all_keys.shape[1]
    steps_new = queries.shape[1]
    scores = jnp.einsum(
        "rqhd,rkhd->rhqk", queries, all_keys, preferred_element_type=jnp.float32
    ) / math.sqrt(HD)
    distance = (prefix_len + jnp.arange(steps_new, dtype=jnp.int32))[:, None] - jnp.arange(
        span, dtype=jnp.int32
    )[None, :]
    scores = scores - slopes[None, :, None, None] * distance.astype(jnp.float32)[None, None]
    scores = jnp.where((distance >= 0)[None, None], scores, -jnp.inf)
    row_max = jnp.max(scores, axis=-1, keepdims=True)
    raised = jnp.exp(scores - row_max)
    weights = (raised / jnp.sum(raised, axis=-1, keepdims=True)).astype(jnp.bfloat16)
    return jnp.einsum(
        "rhqk,rkhd->rqhd", weights, all_values, preferred_element_type=jnp.float32
    ).astype(jnp.bfloat16)


def per_device(
    tokens, ln_gain, ln_bias, w_qkv, qkv_bias, w_dense, dense_bias, prefix_kv, lengths, owner_slot
):
    shards = lax.axis_size("req")
    req_rank = lax.axis_index("req")
    tp_rank = lax.axis_index("tp")
    tok_dev, part_cols = tokens.shape
    reqs_dev = lengths.shape[1]
    per_peer = max(1, reqs_dev // shards)
    buckets = shards * per_peer
    head_cols = w_dense.shape[0]
    heads_here = head_cols // HD
    slot_ids = jnp.arange(reqs_dev, dtype=jnp.int32)
    positions = jnp.arange(LMAX, dtype=jnp.int32)
    owners = (owner_slot // reqs_dev).reshape(shards, reqs_dev)
    own_sizes = lax.dynamic_index_in_dim(lengths, req_rank, 0, keepdims=False)
    own_starts = jnp.cumsum(own_sizes) - own_sizes
    own_dest = lax.dynamic_index_in_dim(owners, req_rank, 0, keepdims=False)
    send_bucket = own_dest * per_peer + slot_ids // shards
    send_table = bucket_table(send_bucket, buckets)
    bucket_start = jnp.sum(send_table * own_starts[None, :], axis=1)
    bucket_size = jnp.sum(send_table * own_sizes[None, :], axis=1)
    row_index = jnp.minimum(bucket_start[:, None] + positions[None, :], tok_dev - 1).reshape(-1)
    row_valid = (positions[None, :] < bucket_size[:, None]).reshape(-1, 1)
    outgoing = jnp.where(
        row_valid, jnp.take(tokens, row_index, axis=0), jnp.zeros((), tokens.dtype)
    )
    incoming = lax.all_to_all(
        outgoing.reshape(shards, per_peer * LMAX, part_cols),
        "req",
        split_axis=0,
        concat_axis=0,
        tiled=True,
    )
    owned_here = (owners == req_rank).astype(jnp.int32)
    source_of = jnp.sum(owned_here * jnp.arange(shards, dtype=jnp.int32)[:, None], axis=0)
    slot_sizes = jnp.sum(owned_here * lengths, axis=0)
    arrival = source_of * per_peer + slot_ids // shards
    slot_rows = (arrival[:, None] * LMAX + positions[None, :]).reshape(-1)
    local_rows = jnp.take(incoming.reshape(-1, part_cols), slot_rows, axis=0)
    slot_valid = positions[None, :] < slot_sizes[:, None]
    qkv_matrix = w_qkv.reshape(w_qkv.shape[0], -1)
    count_rows = reqs_dev * LMAX
    whole_rows, whole_gain, whole_shift = (
        lax.all_gather(local_rows, "tp", axis=1, tiled=True),
        lax.all_gather(ln_gain, "tp", axis=0, tiled=True),
        lax.all_gather(ln_bias, "tp", axis=0, tiled=True),
    )
    values = whole_rows.astype(jnp.float32)
    normed = moments_norm(
        values,
        jnp.sum(values, axis=1),
        jnp.sum(values * values, axis=1),
        whole_gain,
        whole_shift,
        D,
    )
    projected = jnp.dot(normed, qkv_matrix, preferred_element_type=jnp.float32)
    projected = (projected + qkv_bias.reshape(-1).astype(jnp.float32)).reshape(
        reqs_dev, LMAX, 3, heads_here, HD
    )
    live_mask = slot_valid[:, :, None, None]
    queries = projected[:, :, 0].astype(jnp.bfloat16)
    new_keys = jnp.where(live_mask, projected[:, :, 1], 0.0).astype(jnp.bfloat16)
    new_vals = jnp.where(live_mask, projected[:, :, 2], 0.0).astype(jnp.bfloat16)
    stored = prefix_kv.reshape(reqs_dev, PRE, 2, heads_here, HD)
    all_keys = jnp.concatenate([stored[:, :, 0], new_keys], axis=1)
    all_values = jnp.concatenate([stored[:, :, 1], new_vals], axis=1)
    head_ids = tp_rank * heads_here + jnp.arange(heads_here, dtype=jnp.int32) + 1
    slopes = jnp.exp2(-4.0 * head_ids.astype(jnp.float32) / HEADS)
    context = attend(queries, all_keys, all_values, slopes, PRE)
    new_cache = jnp.stack(
        [new_keys.reshape(reqs_dev, LMAX, head_cols), new_vals.reshape(reqs_dev, LMAX, head_cols)],
        axis=2,
    )
    flat_context = context.reshape(count_rows, head_cols)
    back_table = bucket_table(arrival, buckets)
    back_slot = jnp.sum(back_table * slot_ids[None, :], axis=1)
    back_rows = (back_slot[:, None] * LMAX + positions[None, :]).reshape(-1)
    tok_ids = jnp.arange(tok_dev, dtype=jnp.int32)
    token_req = jnp.sum((tok_ids[:, None] >= own_starts[None, :]).astype(jnp.int32), axis=1) - 1
    req_table = (token_req[:, None] == slot_ids[None, :]).astype(jnp.int32)
    home_index = jnp.sum(req_table * (send_bucket * LMAX - own_starts)[None, :], axis=1) + tok_ids
    partial_value = jnp.dot(flat_context, w_dense, preferred_element_type=jnp.float32)
    summed = lax.psum_scatter(
        partial_value.astype(jnp.bfloat16), "tp", scatter_dimension=1, tiled=True
    ).astype(jnp.float32)
    finished = (summed + dense_bias.astype(jnp.float32)).astype(jnp.bfloat16)
    outbound = jnp.take(finished, back_rows, axis=0).reshape(
        shards, per_peer * LMAX, finished.shape[1]
    )
    returned = lax.all_to_all(outbound, "req", split_axis=0, concat_axis=0, tiled=True)
    output = jnp.take(returned.reshape(-1, returned.shape[2]), home_index, axis=0)
    return (output, new_cache)


def solution(mesh):
    return jax.shard_map(
        per_device,
        mesh=mesh,
        in_specs=(
            P("req", "tp"),
            P("tp"),
            P("tp"),
            P(None, None, "tp"),
            P(None, "tp"),
            P("tp", None),
            P("tp"),
            P("req", None, None, "tp"),
            P(),
            P(),
        ),
        out_specs=(P("req", "tp"), P("req", None, None, "tp")),
        check_vma=False,
    )
```

profile of v0, /device:TPU:1, one launch (start us, length us, event | category | flops | bytes accessed | tf_op | source)
XLA Modules:
  0.0 178.7 jit_solution(6938996766615749987)
XLA Ops:
  7.2 0.9 copy.35
  8.3 0.7 add_select_fusion
  9.5 3.9 %gather_fusion = bf16[1024,256]{1,0:T(8,128)(2,1)S(1)} fusion(bf16[208,256]{1,0:T(8,128)(2,1)S(1)} %copy-done.1, s32[1024]{0:T(1024)S(1)} %broadcast_clamp_fusion.1), kind=kCustom, calls=%fused_computation | custom fusion | bytes 1052672 | tf_op jit(solution)/shard_map/jit(_take)/gather | solution.py:72
  13.4 1.1 select_select_fusion
  14.6 11.7 %all-to-all-start = ((bf16[64,16,256]{2,1,0:T(8,128)(2,1)}), bf16[64,16,256]{2,1,0:T(8,128)(2,1)S(1)}, u32[]{:S(2)}, u32[]{:S(2)}) async-start(bf16[64,16,256]{2,1,0:T(8,128)(2,1)} %select_select_fusion), calls=%async_computation | async-start | bytes 1048576 | tf_op jit(solution)/shard_map/all_to_all | solution.py:74
  26.7 17.3 %all-to-all-done = bf16[64,16,256]{2,1,0:T(8,128)(2,1)S(1)} async-done(((bf16[64,16,256]{2,1,0:T(8,128)(2,1)}), bf16[64,16,256]{2,1,0:T(8,128)(2,1)S(1)}, u32[]{:S(2)}, u32[]{:S(2)}) %all-to-all-start) | async-done | bytes 524320 | tf_op jit(solution)/shard_map/all_to_all | solution.py:74
  44.0 1.2 gather_fusion.1
  45.2 0.8 broadcast_select_fusion.1
  46.0 1.6 copy.38
  47.6 18.9 %all-gather = bf16[8,1,256]{2,1,0:T(2,128)(2,1)S(1)} all-gather(bf16[1,1,256]{2,1,0:T(2,128)(2,1)S(1)} %reshape.492), channel_id=1, replica_groups=mesh['req'=64,'tp'=8] {'tp'}, dimensions={0}, use_global_device_ids=true | all-gather | bytes 4608 | tf_op jit(solution)/shard_map/all_gather | solution.py:92
  66.5 10.7 %all-gather.1 = bf16[8,1,256]{2,1,0:T(2,128)(2,1)S(1)} all-gather(bf16[1,1,256]{2,1,0:T(2,128)(2,1)S(1)} %reshape.494), channel_id=1, replica_groups=mesh['req'=64,'tp'=8] {'tp'}, dimensions={0}, use_global_device_ids=true | all-gather | bytes 4608 | tf_op jit(solution)/shard_map/all_gather | solution.py:93
  77.6 6.5 %all-gather.4.cloned.1.call-done = bf16[256,2048]{1,0:T(8,128)(2,1)} async-done(((bf16[256,256]{1,0:T(8,128)(2,1)}), bf16[256,2048]{1,0:T(8,128)(2,1)}) %all-gather.4.cloned.1.call-update) | async-done | bytes 1048592 | tf_op jit(solution)/shard_map/all_gather | solution.py:91
  84.1 1.7 convert_reduce_fusion
  85.8 2.0 %convolution_add_fusion = bf16[256,384]{1,0:T(8,128)(2,1)S(1)} fusion(bf16[2048,384]{0,1:T(8,128)(2,1)S(1)} %bitcast.64, bf16[256,2048]{1,0:T(8,128)(2,1)} %all-gather.4.cloned.1.call-done, f32[2048]{0:T(1024)S(1)} %bitcast.70, f32[2048]{0:T(1024)S(1)} %bitcast.69, f32[256]{0:T(256)S(1)} %get-tuple-element.28, f32[256]{0:T(256)S(1)} %get-tuple-element.27, ...), kind=kOutput, calls=%fused_computation.14 | convolution fusion | flops 405995520 | bytes 2838016 | tf_op jit(solution)/shard_map/dot_general | solution.py:104
  89.2 1.4 convolution_convert_fusion
  91.1 40.7 %reduce-scatter.2.cloned.1.call-done = bf16[256,256]{1,0:T(8,128)(2,1)} async-done(((bf16[256,2048]{1,0:T(8,128)(2,1)}), bf16[256,256]{1,0:T(8,128)(2,1)}) %reduce-scatter.2.cloned.1.call-update) | async-done | bytes 131088 | tf_op jit(solution)/shard_map/reduce_scatter | solution.py:131
  131.8 0.9 add_convert_fusion
  132.7 3.9 %gather_fusion.2 = bf16[1024,256]{1,0:T(8,128)(2,1)S(1)} fusion(bf16[256,256]{1,0:T(8,128)(2,1)S(1)} %add_convert_fusion, s32[1024]{0:T(1024)S(1)} %broadcast_clamp_fusion), kind=kCustom, calls=%fused_computation.2 | custom fusion | bytes 1052672 | tf_op jit(solution)/shard_map/jit(_take)/gather | solution.py:135
  136.7 1.0 broadcast_select_fusion
  137.7 14.8 %all-to-all-start.1 = ((bf16[64,16,256]{2,1,0:T(8,128)(2,1)}), bf16[64,16,256]{2,1,0:T(8,128)(2,1)S(1)}, u32[]{:S(2)}, u32[]{:S(2)}) async-start(bf16[64,16,256]{2,1,0:T(8,128)(2,1)} %broadcast_select_fusion), calls=%async_computation.2 | async-start | bytes 1048576 | tf_op jit(solution)/shard_map/all_to_all | solution.py:138
  152.7 0.8 copy.42
  153.5 16.6 %all-to-all-done.1 = bf16[64,16,256]{2,1,0:T(8,128)(2,1)S(1)} async-done(((bf16[64,16,256]{2,1,0:T(8,128)(2,1)}), bf16[64,16,256]{2,1,0:T(8,128)(2,1)S(1)}, u32[]{:S(2)}, u32[]{:S(2)}) %all-to-all-start.1) | async-done | bytes 524320 | tf_op jit(solution)/shard_map/all_to_all | solution.py:138
  170.1 1.0 gather_fusion.3
  171.2 0.7 broadcast_select_fusion.2
  (74 shorter events, 3.4 us)
Async XLA Ops:
  7.2 82.0 %copy-start = (bf16[128,2048]{1,0:T(8,128)(2,1)S(1)}, bf16[128,2048]{1,0:T(8,128)(2,1)}, u32[]{:S(2)}) copy-start(bf16[128,2048]{1,0:T(8,128)(2,1)} %param.15) | copy-start | bytes 1572868
  7.2 2.3 %copy-start.1 = (bf16[208,256]{1,0:T(8,128)(2,1)S(1)}, bf16[208,256]{1,0:T(8,128)(2,1)}, u32[]{:S(2)}) copy-start(bf16[208,256]{1,0:T(8,128)(2,1)} %param.10) | copy-start | bytes 319492
  14.6 31.5 %copy-start.2 = (bf16[2048,3,128]{2,0,1:T(8,128)(2,1)S(1)}, bf16[2048,3,128]{2,0,1:T(8,128)(2,1)}, u32[]{:S(2)}) copy-start(bf16[2048,3,128]{2,0,1:T(8,128)(2,1)} %param.13) | copy-start | bytes 4718596
  14.6 29.4 %all-to-all-start = ((bf16[64,16,256]{2,1,0:T(8,128)(2,1)}), bf16[64,16,256]{2,1,0:T(8,128)(2,1)S(1)}, u32[]{:S(2)}, u32[]{:S(2)}) async-start(bf16[64,16,256]{2,1,0:T(8,128)(2,1)} %select_select_fusion), calls=%async_computation | async-start | bytes 1048576 | tf_op jit(solution)/shard_map/all_to_all | solution.py:74
  26.3 57.8 %all-gather.4.cloned.1.call-start = ((), (), s32[]{:S(2)}) async-start(), calls=%async_computation.3 | async-start | bytes 1179648 | tf_op jit(solution)/shard_map/all_gather | solution.py:91
  45.9 1.7 copy-start.6
  45.9 20.6 %copy-start.7 = (bf16[256]{0:T(256)(128)(2,1)S(1)}, bf16[256]{0:T(256)(128)(2,1)}, u32[]{:S(2)}) copy-start(bf16[256]{0:T(256)(128)(2,1)} %param.12) | copy-start | bytes 1540
  46.0 31.3 %copy-start.4 = (bf16[16,32,2,128]{3,2,1,0:T(2,128)(2,1)S(1)}, bf16[16,32,2,128]{3,2,1,0:T(2,128)(2,1)}, u32[]{:S(2)}) copy-start(bf16[16,32,2,128]{3,2,1,0:T(2,128)(2,1)} %param.17) | copy-start | bytes 786436
  46.0 31.5 %copy-start.5 = (bf16[3,128]{1,0:T(4,128)(2,1)S(1)}, bf16[3,128]{1,0:T(4,128)(2,1)}, u32[]{:S(2)}) copy-start(bf16[3,128]{1,0:T(4,128)(2,1)} %param.14) | copy-start | bytes 2308
  46.0 85.8 %reduce-scatter.2.cloned.1.call-start = ((), (), s32[]{:S(2)}) async-start(), calls=%async_computation.4 | async-start | bytes 1179648 | tf_op jit(solution)/shard_map/reduce_scatter | solution.py:131
  47.6 38.2 %copy-start.3 = (bf16[2048,3,128]{0,2,1:T(8,128)(2,1)S(1)}, bf16[2048,3,128]{0,2,1:T(8,128)(2,1)}, u32[]{:S(2)}) copy-start(bf16[2048,3,128]{0,2,1:T(8,128)(2,1)} %copy.38) | copy-start | bytes 4718596
  88.7 2.0 %copy-start.8 = (bf16[256]{0:T(256)(128)(2,1)S(1)}, bf16[256]{0:T(256)(128)(2,1)}, u32[]{:S(2)}) copy-start(bf16[256]{0:T(256)(128)(2,1)} %param.16) | copy-start | bytes 1540
  137.7 32.5 %all-to-all-start.1 = ((bf16[64,16,256]{2,1,0:T(8,128)(2,1)}), bf16[64,16,256]{2,1,0:T(8,128)(2,1)S(1)}, u32[]{:S(2)}, u32[]{:S(2)}) async-start(bf16[64,16,256]{2,1,0:T(8,128)(2,1)} %broadcast_select_fusion), calls=%async_computation.2 | async-start | bytes 1048576 | tf_op jit(solution)/shard_map/all_to_all | solution.py:138
Sparse Core Ops, SparseCore 0:
  46.1 37.9 all-gather.3
  90.8 40.9 reduce-scatter.1
where the time goes:
time: 179 us
  waiting for transfers between devices  81.2 us (45%)
  blocking collectives  29.5 us (16%)
  starting transfers between devices  26.6 us (15%)
  between operations  14.4 us (8%)
  local copies, waits for them, and re-layouts  14.2 us (8%)
  other arithmetic  8.64 us (5%)
  matrix products  4.15 us (2%)
    reduce_scatter x1, waiting for transfers between devices, per_device(): lax.psum_scatter(partial_value.astype(jnp.bfloat16), 'tp', scatter_dimens...  40.7 us
    all_gather x1, blocking collectives, per_device(): lax.all_gather(ln_gain, 'tp', axis=0, tiled=True)  18.9 us
    all_to_all x1, waiting for transfers between devices, per_device(): lax.all_to_all(outgoing.reshape(shards, per_peer * LMAX, part_cols), 'req...  17.3 us
    all_to_all x1, waiting for transfers between devices, per_device(): lax.all_to_all(outbound, 'req', split_axis=0, concat_axis=0, tiled=True)  16.6 us
    all_to_all x1, starting transfers between devices, per_device(): lax.all_to_all(outbound, 'req', split_axis=0, concat_axis=0, tiled=True)  14.8 us
    all_to_all x1, starting transfers between devices, per_device(): lax.all_to_all(outgoing.reshape(shards, per_peer * LMAX, part_cols), 'req...  11.7 us
    all_gather x1, blocking collectives, per_device(): lax.all_gather(ln_bias, 'tp', axis=0, tiled=True)  10.7 us
    all_gather x1, waiting for transfers between devices, per_device(): lax.all_gather(local_rows, 'tp', axis=1, tiled=True)  6.51 us
  transfers between devices with their start and end apart: 4, of which 4 were waited for; matrix products, arithmetic and copies ran while one was open for 2% of the time, Pallas kernels for 0%

commit v1 on v0

--- a/solution.py
+++ b/solution.py
@@ -90,7 +90,9 @@
     whole_rows, whole_gain, whole_shift = (
         lax.all_gather(local_rows, "tp", axis=1, tiled=True),
         lax.all_gather(ln_gain, "tp", axis=0, tiled=True),
-        lax.all_gather(ln_bias, "tp", axis=0, tiled=True),
+        jnp.concatenate(
+            lax.all_to_all(jnp.stack([ln_bias] * lax.axis_size("tp")), "tp", 0, 0), axis=0
+        ),
     )
     values = whole_rows.astype(jnp.float32)
     normed = moments_norm(

time: 179 us -> 180 us (level)
  blocking collectives: 29.5 us -> 13 us
  starting transfers between devices: 26.6 us -> 36.8 us
  waiting for transfers between devices: 81.2 us -> 85.8 us
    all_gather x1 -> x0, blocking collectives: 10.7 us -> none  [per_device(): lax.all_gather(ln_bias, 'tp', axis=0, tiled=True)]
    all_to_all x0 -> x1, starting transfers between devices: none -> 10 us  [per_device(): lax.all_to_all(jnp.stack([ln_bias] * lax.axis_size('tp')), 'tp', 0, 0)]
    all_gather x1, blocking collectives: 18.9 us -> 13 us  [per_device(): lax.all_gather(ln_gain, 'tp', axis=0, tiled=True)]
    all_gather x1, waiting for transfers between devices: 6.51 us -> 11.2 us  [per_device(): lax.all_gather(local_rows, 'tp', axis=1, tiled=True)]
    unnamed x24 -> x23, local copies, waits for them, and re-layouts: 3.34 us -> 3.94 us
  transfers between devices with their start and end apart: 4 -> 5, of which waited for: 4 -> 4; matrix products, arithmetic and copies ran while one was open for 2% -> 3% of each run, Pallas kernels for 0% -> 0%
where the time goes in v1:
time: 180 us; the launch traced here: 179 us
  waiting for transfers between devices  85.8 us (48%)
  starting transfers between devices  36.8 us (20%)
  local copies, waits for them, and re-layouts  15.3 us (8%)
  between operations  14.4 us (8%)
  blocking collectives  13 us (7%)
  other arithmetic  9.31 us (5%)
  matrix products  4.66 us (3%)
    reduce_scatter x1, waiting for transfers between devices, per_device(): lax.psum_scatter(partial_value.astype(jnp.bfloat16), 'tp', scatter_dimens...  40.7 us
    all_to_all x1, waiting for transfers between devices, per_device(): lax.all_to_all(outgoing.reshape(shards, per_peer * LMAX, part_cols), 'req...  17.3 us
    all_to_all x1, waiting for transfers between devices, per_device(): lax.all_to_all(outbound, 'req', split_axis=0, concat_axis=0, tiled=True)  16.6 us
    all_to_all x1, starting transfers between devices, per_device(): lax.all_to_all(outbound, 'req', split_axis=0, concat_axis=0, tiled=True)  15 us
    all_gather x1, blocking collectives, per_device(): lax.all_gather(ln_gain, 'tp', axis=0, tiled=True)  13 us
    all_to_all x1, starting transfers between devices, per_device(): lax.all_to_all(outgoing.reshape(shards, per_peer * LMAX, part_cols), 'req...  11.7 us
    all_gather x1, waiting for transfers between devices, per_device(): lax.all_gather(local_rows, 'tp', axis=1, tiled=True)  11.2 us
    all_to_all x1, starting transfers between devices, per_device(): lax.all_to_all(jnp.stack([ln_bias] * lax.axis_size('tp')), 'tp', 0, 0)  10 us
  transfers between devices with their start and end apart: 5, of which 4 were waited for; matrix products, arithmetic and copies ran while one was open for 3% of the time, Pallas kernels for 0%

profile of v1, /device:TPU:1, one launch (start us, length us, event | category | flops | bytes accessed | tf_op | source)
XLA Modules:
  0.0 179.4 jit_solution(2692311006052857599)
XLA Ops:
  7.2 0.9 copy.35
  8.3 0.7 add_select_fusion
  9.5 3.9 %gather_fusion = bf16[1024,256]{1,0:T(8,128)(2,1)S(1)} fusion(bf16[208,256]{1,0:T(8,128)(2,1)S(1)} %copy-done.1, s32[1024]{0:T(1024)S(1)} %broadcast_clamp_fusion.1), kind=kCustom, calls=%fused_computation | custom fusion | bytes 1052672 | tf_op jit(solution)/shard_map/jit(_take)/gather | solution.py:72
  13.4 1.1 select_select_fusion
  14.6 11.7 %all-to-all-start = ((bf16[64,16,256]{2,1,0:T(8,128)(2,1)}), bf16[64,16,256]{2,1,0:T(8,128)(2,1)S(1)}, u32[]{:S(2)}, u32[]{:S(2)}) async-start(bf16[64,16,256]{2,1,0:T(8,128)(2,1)} %select_select_fusion), calls=%async_computation | async-start | bytes 1048576 | tf_op jit(solution)/shard_map/all_to_all | solution.py:74
  26.7 17.3 %all-to-all-done = bf16[64,16,256]{2,1,0:T(8,128)(2,1)S(1)} async-done(((bf16[64,16,256]{2,1,0:T(8,128)(2,1)}), bf16[64,16,256]{2,1,0:T(8,128)(2,1)S(1)}, u32[]{:S(2)}, u32[]{:S(2)}) %all-to-all-start) | async-done | bytes 524320 | tf_op jit(solution)/shard_map/all_to_all | solution.py:74
  44.0 1.2 gather_fusion.1
  45.2 0.8 broadcast_select_fusion.1
  47.8 10.0 %all-to-all-start.1 = ((bf16[8,2,128]{2,1,0:T(2,128)(2,1)}), bf16[8,2,128]{2,1,0:T(2,128)(2,1)S(1)}, u32[]{:S(2)}, u32[]{:S(2)}) async-start(bf16[8,2,128]{2,1,0:T(2,128)(2,1)} %reshape.511), calls=%async_computation.1 | async-start | bytes 8192 | tf_op jit(solution)/shard_map/all_to_all | solution.py:94
  58.2 1.6 copy.38
  59.8 13.0 %all-gather = bf16[8,1,256]{2,1,0:T(2,128)(2,1)S(1)} all-gather(bf16[1,1,256]{2,1,0:T(2,128)(2,1)S(1)} %reshape.508), channel_id=1, replica_groups=mesh['req'=64,'tp'=8] {'tp'}, dimensions={0}, use_global_device_ids=true | all-gather | bytes 4608 | tf_op jit(solution)/shard_map/all_gather | solution.py:92
  72.8 11.2 %all-gather.3.cloned.1.call-done = bf16[256,2048]{1,0:T(8,128)(2,1)} async-done(((bf16[256,256]{1,0:T(8,128)(2,1)}), bf16[256,2048]{1,0:T(8,128)(2,1)}) %all-gather.3.cloned.1.call-update) | async-done | bytes 1048592 | tf_op jit(solution)/shard_map/all_gather | solution.py:91
  84.0 1.7 convert_reduce_fusion
  85.7 2.5 %convolution_add_fusion = bf16[256,384]{1,0:T(8,128)(2,1)S(1)} fusion(bf16[2048,384]{0,1:T(8,128)(2,1)} %bitcast.64, bf16[256,2048]{1,0:T(8,128)(2,1)} %all-gather.3.cloned.1.call-done, f32[2048]{0:T(1024)S(1)} %bitcast.70, f32[2048]{0:T(1024)S(1)} %bitcast.69, f32[256]{0:T(256)S(1)} %get-tuple-element.28, f32[256]{0:T(256)S(1)} %get-tuple-element.27, ...), kind=kOutput, calls=%fused_computation.14 | convolution fusion | flops 405995520 | bytes 2838016 | tf_op jit(solution)/shard_map/dot_general | solution.py:106
  89.6 1.4 convolution_convert_fusion
  91.5 40.7 %reduce-scatter.2.cloned.1.call-done = bf16[256,256]{1,0:T(8,128)(2,1)} async-done(((bf16[256,2048]{1,0:T(8,128)(2,1)}), bf16[256,256]{1,0:T(8,128)(2,1)}) %reduce-scatter.2.cloned.1.call-update) | async-done | bytes 131088 | tf_op jit(solution)/shard_map/reduce_scatter | solution.py:133
  132.2 0.9 add_convert_fusion
  133.1 3.9 %gather_fusion.2 = bf16[1024,256]{1,0:T(8,128)(2,1)S(1)} fusion(bf16[256,256]{1,0:T(8,128)(2,1)S(1)} %add_convert_fusion, s32[1024]{0:T(1024)S(1)} %broadcast_clamp_fusion), kind=kCustom, calls=%fused_computation.2 | custom fusion | bytes 1052672 | tf_op jit(solution)/shard_map/jit(_take)/gather | solution.py:137
  137.1 1.0 broadcast_select_fusion
  138.1 15.0 %all-to-all-start.2 = ((bf16[64,16,256]{2,1,0:T(8,128)(2,1)}), bf16[64,16,256]{2,1,0:T(8,128)(2,1)S(1)}, u32[]{:S(2)}, u32[]{:S(2)}) async-start(bf16[64,16,256]{2,1,0:T(8,128)(2,1)} %broadcast_select_fusion), calls=%async_computation.3 | async-start | bytes 1048576 | tf_op jit(solution)/shard_map/all_to_all | solution.py:140
  153.3 0.8 copy.42
  154.1 16.6 %all-to-all-done.2 = bf16[64,16,256]{2,1,0:T(8,128)(2,1)S(1)} async-done(((bf16[64,16,256]{2,1,0:T(8,128)(2,1)}), bf16[64,16,256]{2,1,0:T(8,128)(2,1)S(1)}, u32[]{:S(2)}, u32[]{:S(2)}) %all-to-all-start.2) | async-done | bytes 524320 | tf_op jit(solution)/shard_map/all_to_all | solution.py:140
  170.7 1.0 gather_fusion.3
  171.8 0.7 broadcast_select_fusion.2
  (77 shorter events, 5.2 us)
Async XLA Ops:
  7.2 82.5 %copy-start = (bf16[128,2048]{1,0:T(8,128)(2,1)S(1)}, bf16[128,2048]{1,0:T(8,128)(2,1)}, u32[]{:S(2)}) copy-start(bf16[128,2048]{1,0:T(8,128)(2,1)} %param.15) | copy-start | bytes 1572868
  7.2 2.3 %copy-start.1 = (bf16[208,256]{1,0:T(8,128)(2,1)S(1)}, bf16[208,256]{1,0:T(8,128)(2,1)}, u32[]{:S(2)}) copy-start(bf16[208,256]{1,0:T(8,128)(2,1)} %param.10) | copy-start | bytes 319492
  14.6 31.4 %copy-start.5 = (bf16[256]{0:T(256)(128)(2,1)S(1)}, bf16[256]{0:T(256)(128)(2,1)}, u32[]{:S(2)}) copy-start(bf16[256]{0:T(256)(128)(2,1)} %param.12) | copy-start | bytes 1540
  14.6 43.3 %copy-start.3 = (bf16[16,32,2,128]{3,2,1,0:T(2,128)(2,1)S(1)}, bf16[16,32,2,128]{3,2,1,0:T(2,128)(2,1)}, u32[]{:S(2)}) copy-start(bf16[16,32,2,128]{3,2,1,0:T(2,128)(2,1)} %param.17) | copy-start | bytes 786436
  14.6 43.5 %copy-start.4 = (bf16[3,128]{1,0:T(4,128)(2,1)S(1)}, bf16[3,128]{1,0:T(4,128)(2,1)}, u32[]{:S(2)}) copy-start(bf16[3,128]{1,0:T(4,128)(2,1)} %param.14) | copy-start | bytes 2308
  14.6 29.4 %all-to-all-start = ((bf16[64,16,256]{2,1,0:T(8,128)(2,1)}), bf16[64,16,256]{2,1,0:T(8,128)(2,1)S(1)}, u32[]{:S(2)}, u32[]{:S(2)}) async-start(bf16[64,16,256]{2,1,0:T(8,128)(2,1)} %select_select_fusion), calls=%async_computation | async-start | bytes 1048576 | tf_op jit(solution)/shard_map/all_to_all | solution.py:74
  26.3 31.9 %copy-start.2 = (bf16[2048,3,128]{2,0,1:T(8,128)(2,1)S(1)}, bf16[2048,3,128]{2,0,1:T(8,128)(2,1)}, u32[]{:S(2)}) copy-start(bf16[2048,3,128]{2,0,1:T(8,128)(2,1)} %param.13) | copy-start | bytes 4718596
  26.3 57.7 %all-gather.3.cloned.1.call-start = ((), (), s32[]{:S(2)}) async-start(), calls=%async_computation.4 | async-start | bytes 1179648 | tf_op jit(solution)/shard_map/all_gather | solution.py:91
  47.8 25.0 %all-to-all-start.1 = ((bf16[8,2,128]{2,1,0:T(2,128)(2,1)}), bf16[8,2,128]{2,1,0:T(2,128)(2,1)S(1)}, u32[]{:S(2)}, u32[]{:S(2)}) async-start(bf16[8,2,128]{2,1,0:T(2,128)(2,1)} %reshape.511), calls=%async_computation.1 | async-start | bytes 8192 | tf_op jit(solution)/shard_map/all_to_all | solution.py:94
  57.8 74.4 %reduce-scatter.2.cloned.1.call-start = ((), (), s32[]{:S(2)}) async-start(), calls=%async_computation.5 | async-start | bytes 1179648 | tf_op jit(solution)/shard_map/reduce_scatter | solution.py:133
  58.2 1.6 copy-start.6
  89.1 2.0 %copy-start.7 = (bf16[256]{0:T(256)(128)(2,1)S(1)}, bf16[256]{0:T(256)(128)(2,1)}, u32[]{:S(2)}) copy-start(bf16[256]{0:T(256)(128)(2,1)} %param.16) | copy-start | bytes 1540
  138.1 32.7 %all-to-all-start.2 = ((bf16[64,16,256]{2,1,0:T(8,128)(2,1)}), bf16[64,16,256]{2,1,0:T(8,128)(2,1)S(1)}, u32[]{:S(2)}, u32[]{:S(2)}) async-start(bf16[64,16,256]{2,1,0:T(8,128)(2,1)} %broadcast_select_fusion), calls=%async_computation.3 | async-start | bytes 1048576 | tf_op jit(solution)/shard_map/all_to_all | solution.py:140
Sparse Core Ops, SparseCore 0:
  46.1 37.9 all-gather.2
  91.2 40.9 reduce-scatter.1
